TPU v7x, 32 devices: a whole 2x2x4 slice. The times are simulated.
32 devices in a mesh: gx: 8 (over z, x), gy: 4 (over y, core).
Axes of the slice: x: 2, y: 2, z: 4, core: 2. Of those that a mesh axis runs over, the one named last changes fastest.
Arguments:
- velocity: float32 [3, 64, 256, 128], P(None, 'gx', 'gy'), may hold values from -2 to 3, as said below
- counts: int32 [8, 4, 9], P('gx', 'gy'), may hold values from 1 to 1024, as said below
- src_cell: int32 [8, 4, 9, 1024], P('gx', 'gy'), may hold values from 0 to 65535
- weights: float32 [8, 4, 9, 1024], P('gx', 'gy'), may hold values from 0.05 to 0.35
- dst_cell: int32 [8, 4, 9, 1024], P('gx', 'gy'), may hold values from 0 to 65535
- blade_tile: int32 [20, 192], replicated, may hold values from 0 to 31, as said below
- blade_cell: int32 [20, 192], replicated, may hold values from 0 to 65535
- blade_coef: float32 [20, 192], replicated, may hold values from 0.5 to 2
Outputs:
- updated: float32 [3, 64, 256, 128], P(None, 'gx', 'gy')
- forcing: float32 [3, 64, 256, 128], P(None, 'gx', 'gy')
Inputs may be any that keep to these rules, and one draw needn't show every extreme that they name: The velocity components, streamwise with a mean near 1. `counts`: some list is full, with 1024 used slots. `blade_tile`: turbines stand near one spanwise row of tiles; a turbine's points lie in at most three tiles.
All inputs are finite; a program needn't handle non-finite values.
Results may differ from a plain program's by a relative error of at most 0.00002.
Values sent between devices are 32-bit elements; how exact they have to be, the bound alone decides.
No kernel may reach another device: no remote copies, remote signals or barrier semaphores. Data moves between devices by JAX's collectives and lax.ppermute only.
A program may use at most 256 MiB of HBM per device.

v0:
```python
import jax
import jax.numpy as jnp
from jax import lax
from jax.sharding import PartitionSpec as P


def padded_2(cells, sides, width):
    for axis, dim in sides:
        count = lax.axis_size(axis)
        head = lax.slice_in_dim(cells, 0, width, axis=dim)
        tail = lax.slice_in_dim(cells, cells.shape[dim] - width, cells.shape[dim], axis=dim)
        cells = jnp.concatenate(
            [
                lax.ppermute(tail, axis, [(i, (i + 1) % count) for i in range(count)]),
                cells,
                lax.ppermute(head, axis, [((i + 1) % count, i) for i in range(count)]),
            ],
            axis=dim,
        )
    return cells


def body(velocity, counts, src_cell, weights, dst_cell, blade_tile, blade_cell, blade_coef):
    components = velocity.shape[0]
    cells_x = velocity.shape[1]
    cells_y = velocity.shape[2]
    levels = velocity.shape[3]
    total_cells = cells_x * cells_y * levels
    flat_vel = velocity.reshape(components, total_cells)
    count_y = lax.axis_size("gy")
    index_x = lax.axis_index("gx")
    index_y = lax.axis_index("gy")
    my_tile = index_x * count_y + index_y
    sampled = jnp.take(flat_vel, blade_cell, axis=1)
    owned = (blade_tile == my_tile)[None]
    sampled = jnp.where(owned, sampled, jnp.zeros_like(sampled))
    points = blade_cell.shape[1]
    points_x = lax.psum(sampled[0], ("gx", "gy"))
    rotor_mean = jnp.sum(points_x, axis=1) / points
    forces = -blade_coef[None] * rotor_mean[None, :, None] * sampled
    forcing = (
        jnp.zeros((components, total_cells), jnp.float32)
        .at[:, blade_cell.reshape(-1)]
        .add(forces.reshape(components, -1))
    )
    capacity = src_cell.shape[-1]
    active = lax.broadcasted_iota(jnp.int32, (9, capacity), 1) < counts[0, 0][:, None]
    masked_w = jnp.where(active, weights[0, 0], jnp.zeros_like(weights[0, 0]))
    picked = jnp.take(flat_vel, src_cell[0, 0].reshape(-1), axis=1).reshape(components, 9, capacity)
    blocks = jnp.concatenate([picked * masked_w[None], masked_w[None]], axis=0)
    grid_blocks = blocks.reshape(4, 3, 3, capacity)
    bordered = padded_2(grid_blocks, (("gx", 1), ("gy", 2)), 1)
    arrived = bordered[:, ::-2, ::-2].reshape(4, 9, capacity)
    targets = dst_cell[0, 0].reshape(-1)
    totals = jnp.zeros((4, total_cells), jnp.float32).at[:, targets].add(arrived.reshape(4, -1))
    corrected = (1.0 - totals[3]) * flat_vel - totals[:3]
    field_now = corrected.reshape(components, cells_x, cells_y, levels)
    padded = padded_2(field_now, (("gx", 1), ("gy", 2)), 1)
    padded = jnp.pad(padded, ((0, 0), (0, 0), (0, 0), (1, 1)))
    center = padded[:, 1:-1, 1:-1, 1:-1]
    east_side = padded[:, 2:, 1:-1, 1:-1]
    west_side = padded[:, :-2, 1:-1, 1:-1]
    north_side = padded[:, 1:-1, 2:, 1:-1]
    south_side = padded[:, 1:-1, :-2, 1:-1]
    upper_side = padded[:, 1:-1, 1:-1, 2:]
    lower_side = padded[:, 1:-1, 1:-1, :-2]
    laplace = (
        east_side + west_side + north_side + south_side + upper_side + lower_side - 6.0 * center
    )
    advection = (
        center[0:1] * (east_side - west_side) * 0.5
        + center[1:2] * (north_side - south_side) * 0.5
        + center[2:3] * (upper_side - lower_side) * 0.5
    )
    forcing_field = forcing.reshape(components, cells_x, cells_y, levels)
    updated = center + 0.2 * (0.15 * laplace - advection + forcing_field)
    return (updated, forcing_field)


def solution(mesh):
    placed = (
        P(None, "gx", "gy", None),
        P("gx", "gy", None),
        P("gx", "gy", None, None),
        P("gx", "gy", None, None),
        P("gx", "gy", None, None),
        P(),
        P(),
        P(),
    )
    return jax.shard_map(
        body,
        mesh=mesh,
        in_specs=placed,
        out_specs=(P(None, "gx", "gy", None), P(None, "gx", "gy", None)),
        check_vma=False,
    )
```

profile of v0, /device:TPU:1, one launch (start us, length us, event | category | flops | bytes accessed | tf_op | source)
XLA Modules:
  0.0 389.9 jit_solution(10842976870287354699)
XLA Ops:
  0.6 17.6 %copy.47 = f32[3,8,64,128]{0,3,2,1:T(8,128)} copy(f32[3,8,64,128]{3,2,1,0:T(8,128)} %param.8) | data formatting | bytes 1572864 | tf_op args[0]
  18.3 41.5 %gather_fusion = f32[9216,3]{1,0:T(8,128)} fusion(f32[3,65536]{0,1:T(8,128)} %bitcast.38, s32[9216]{0:T(1024)S(1)} %broadcast_clamp_fusion), kind=kCustom, calls=%fused_computation | custom fusion | bytes 258048 | tf_op jit(solution)/shard_map/jit(_take)/gather | solution.py:49
  59.8 3.1 copy.48
  63.5 0.7 reduce.15
  64.7 2.1 collective-permute-start
  66.8 3.1 collective-permute-start.1
  70.1 16.8 %gather_fusion.1 = f32[3840,3]{1,0:T(8,128)S(1)} fusion(f32[3,65536]{0,1:T(8,128)} %bitcast.39, s32[4096]{0:T(1024)S(1)} %pad_clamp_fusion), kind=kCustom, calls=%fused_computation.1 | custom fusion | bytes 107520 | tf_op jit(solution)/shard_map/jit(_take)/gather | solution.py:34
  86.9 0.9 copy.56
  87.8 37.7 %psum.7 = f32[20,192]{1,0:T(8,128)S(1)} all-reduce(f32[20,192]{1,0:T(8,128)S(1)} %fusion.17), channel_id=1, replica_groups=mesh['gx'=8,'gy'=4] {'gx','gy'}, use_global_device_ids=true, to_apply=%region_1.2 | all-reduce | flops 3840 | bytes 30720 | tf_op jit(solution)/shard_map/psum | solution.py:38
  125.8 3.4 collective-permute-start.2
  129.6 1.8 collective-permute-done.2
  131.4 1.6 collective-permute-done.3
  133.2 3.0 copy.49
  136.2 62.9 %scatter_custom_fusion = f32[4,65536]{0,1:T(8,128)} fusion(s32[9216]{0:T(1024)S(1)} %bitcast.52, f32[9216,4]{1,0:T(8,128)} %copy.49, f32[]{:T(128)} %constant.18.clone.1), kind=kCustom, calls=%fused_computation.12 | custom fusion | flops 36864 | bytes 1049088 | tf_op jit(solution)/shard_map/scatter-add | solution.py:55
  199.1 20.3 %fusion = f32[65536]{0:T(1024)S(1)} fusion(f32[4,65536]{0,1:T(8,128)} %scatter_custom_fusion), kind=kLoop, calls=%fused_computation.9 | loop fusion | flops 65536 | bytes 524288 | tf_op jit(solution)/shard_map/sub | solution.py:56
  219.4 34.2 %slice_subtract_fusion = f32[3,65536]{0,1:T(8,128)} fusion(f32[4,65536]{0,1:T(8,128)} %scatter_custom_fusion, f32[65536]{0:T(1024)S(1)} %fusion, f32[3,8,64,128]{0,3,2,1:T(8,128)} %copy.47), kind=kLoop, calls=%fused_computation.7 | loop fusion | flops 393216 | bytes 2621440 | tf_op jit(solution)/shard_map/sub | solution.py:56
  253.6 19.5 %copy.59 = f32[3,8,64,128]{3,2,1,0:T(8,128)S(1)} copy(f32[3,8,64,128]{0,3,2,1:T(8,128)} %bitcast.37) | data formatting | bytes 1572864 | tf_op jit(solution)/shard_map/reshape | solution.py:57
  273.1 2.8 collective-permute-start.4
  276.0 37.5 %scatter_custom_fusion.1 = f32[3,65536]{0,1:T(8,128)} fusion(s32[3840]{0:T(1024)S(1)} %fusion.18, f32[]{:T(128)} %constant.18.clone.1, f32[3840,3]{1,0:T(8,128)S(1)} %gather_fusion.1, f32[]{:T(128)} %constant.22.clone.1, f32[3840]{0:T(1024)S(1)} %mul.117, pred[3840]{0:T(1024)(128)(4,1)S(1)} %broadcast_in_dim.77, pred[3840]{0:T(1024)(128)(4,1)S(1)} %broadcast_in_dim.75), kind=kCustom, calls=%fused_computation.10 | custom fusion | flops 46080 | bytes 2778624 | tf_op jit(solution)/shard_map/scatter-add | solution.py:44
  313.5 19.5 %copy.58 = f32[3,8,64,128]{3,2,1,0:T(8,128)S(1)} copy(f32[3,8,64,128]{0,3,2,1:T(8,128)} %bitcast.40) | data formatting | bytes 1572864 | tf_op jit(solution)/shard_map/reshape | solution.py:75
  333.1 1.7 collective-permute-start.7
  334.8 52.5 %slice_reduce_fusion.2 = (f32[65536]{0:T(1024)S(1)}, f32[65536]{0:T(1024)S(1)}, f32[65536]{0:T(1024)S(1)}) fusion(f32[3,65536]{0,1:T(8,128)} %slice_subtract_fusion), kind=kLoop, calls=%fused_computation.6 | loop fusion | bytes 1572864 | tf_op jit(solution)/shard_map/slice | solution.py:71
  387.3 0.8 select_maximum_fusion
  388.1 1.8 multiply_add_fusion
  (58 shorter events, 2.3 us)
Async XLA Ops:
  0.6 17.6 %copy-start.2 = (s32[1,1,9,1024]{3,1,2,0:T(1,128)S(1)}, s32[1,1,9,1024]{3,1,2,0:T(1,128)}, u32[]{:S(2)}) copy-start(s32[1,1,9,1024]{3,1,2,0:T(1,128)} %param.10) | copy-start | bytes 110596
  18.2 45.3 %copy-start.7 = (s32[1,1,9]{2,1,0:T(1,128)S(1)}, s32[1,1,9]{2,1,0:T(1,128)}, u32[]{:S(2)}) copy-start(s32[1,1,9]{2,1,0:T(1,128)} %param.9) | copy-start | bytes 112
  18.2 46.0 %copy-start.3 = (f32[1,1,9,1024]{3,1,2,0:T(1,128)S(1)}, f32[1,1,9,1024]{3,1,2,0:T(1,128)}, u32[]{:S(2)}) copy-start(f32[1,1,9,1024]{3,1,2,0:T(1,128)} %param.11) | copy-start | bytes 110596
  18.2 51.7 %copy-start.4 = (s32[1,1,9,1024]{3,1,2,0:T(1,128)S(1)}, s32[1,1,9,1024]{3,1,2,0:T(1,128)}, u32[]{:S(2)}) copy-start(s32[1,1,9,1024]{3,1,2,0:T(1,128)} %param.12) | copy-start | bytes 110596
  18.2 51.8 %copy-start.1 = (s32[20,192]{1,0:T(8,128)S(1)}, s32[20,192]{1,0:T(8,128)}, u32[]{:S(2)}) copy-start(s32[20,192]{1,0:T(8,128)} %param.14) | copy-start | bytes 46084
  59.8 28.0 %copy-start.6 = (s32[20,192]{1,0:T(8,128)S(1)}, s32[20,192]{1,0:T(8,128)}, u32[]{:S(2)}) copy-start(s32[20,192]{1,0:T(8,128)} %param.13) | copy-start | bytes 46084
  59.8 69.4 %copy-start.5 = (f32[20,192]{1,0:T(8,128)S(1)}, f32[20,192]{1,0:T(8,128)}, u32[]{:S(2)}) copy-start(f32[20,192]{1,0:T(8,128)} %param.15) | copy-start | bytes 46084
  64.7 61.0 %collective-permute-start = (f32[4,1,3,1024]{3,0,2,1:T(4,128)S(1)}, f32[4,1,3,1024]{3,0,2,1:T(4,128)S(1)}, u32[]{:S(2)}, u32[]{:S(2)}) collective-permute-start(f32[4,1,3,1024]{3,0,2,1:T(4,128)S(1)} %get-tuple-element.19), channel_id=1, source_target_pairs={{0,4},{4,8},{8,12},{12,16},{16,20},{20,24},{24,28},{28,0},{1,5},{5... | collective-permute-start | bytes 147464 | tf_op jit(solution)/shard_map/ppermute | solution.py:14
  66.8 58.9 %collective-permute-start.1 = (f32[4,1,3,1024]{3,0,2,1:T(4,128)S(1)}, f32[4,1,3,1024]{3,0,2,1:T(4,128)S(1)}, u32[]{:S(2)}, u32[]{:S(2)}) collective-permute-start(f32[4,1,3,1024]{3,0,2,1:T(4,128)S(1)} %get-tuple-element.20), channel_id=1, source_target_pairs={{4,0},{8,4},{12,8},{16,12},{20,16},{24,20},{28,24},{0,28},{5,1},{9... | collective-permute-start | bytes 147464 | tf_op jit(solution)/shard_map/ppermute | solution.py:16
  125.8 5.6 %collective-permute-start.2 = (f32[4,5,1,1024]{3,0,2,1:T(4,128)S(1)}, f32[4,5,1,1024]{3,0,2,1:T(4,128)S(1)}, u32[]{:S(2)}, u32[]{:S(2)}) collective-permute-start(f32[4,5,1,1024]{3,0,2,1:T(4,128)S(1)} %get-tuple-element.17), channel_id=1, source_target_pairs={{0,1},{1,2},{2,3},{3,0},{4,5},{5,6},{6,7},{7,4},{8,9},{9,10},{10,1... | collective-permute-start | bytes 245768 | tf_op jit(solution)/shard_map/ppermute | solution.py:14
  129.2 3.9 collective-permute-start.3
  273.1 59.8 %collective-permute-start.4 = (f32[3,1,64,128]{3,2,1,0:T(8,128)S(1)}, f32[3,1,64,128]{3,2,1,0:T(8,128)S(1)}, u32[]{:S(2)}, u32[]{:S(2)}) collective-permute-start(f32[3,1,64,128]{3,2,1,0:T(8,128)S(1)} %get-tuple-element.16), channel_id=1, source_target_pairs={{4,0},{8,4},{12,8},{16,12},{20,16},{24,20},{28,24},{0,28},{5,1},{9... | collective-permute-start | bytes 294920 | tf_op jit(solution)/shard_map/ppermute | solution.py:16
  276.0 57.0 %collective-permute-start.5 = (f32[3,1,64,128]{3,2,1,0:T(8,128)S(1)}, f32[3,1,64,128]{3,2,1,0:T(8,128)S(1)}, u32[]{:S(2)}, u32[]{:S(2)}) collective-permute-start(f32[3,1,64,128]{3,2,1,0:T(8,128)S(1)} %get-tuple-element.15), channel_id=1, source_target_pairs={{0,4},{4,8},{8,12},{12,16},{16,20},{20,24},{24,28},{28,0},{1,5},{5... | collective-permute-start | bytes 294920 | tf_op jit(solution)/shard_map/ppermute | solution.py:14
  333.0 55.2 %copy-start = (f32[3,8,64,128]{3,2,1,0:T(8,128)}, f32[3,8,64,128]{3,2,1,0:T(8,128)S(1)}, u32[]{:S(2)}) copy-start(f32[3,8,64,128]{3,2,1,0:T(8,128)S(1)} %copy.58) | copy-start | bytes 2359300
  333.0 54.3 %collective-permute-start.6 = (f32[3,10,1,128]{3,2,1,0:T(1,128)S(1)}, f32[3,10,1,128]{3,2,1,0:T(1,128)S(1)}, u32[]{:S(2)}, u32[]{:S(2)}) collective-permute-start(f32[3,10,1,128]{3,2,1,0:T(1,128)S(1)} %get-tuple-element.14), channel_id=1, source_target_pairs={{1,0},{2,1},{3,2},{0,3},{5,4},{6,5},{7,6},{4,7},{9,8},{10,9},{11,1... | collective-permute-start | bytes 46088 | tf_op jit(solution)/shard_map/ppermute | solution.py:16
  333.1 54.2 %collective-permute-start.7 = (f32[3,10,1,128]{3,2,1,0:T(1,128)S(1)}, f32[3,10,1,128]{3,2,1,0:T(1,128)S(1)}, u32[]{:S(2)}, u32[]{:S(2)}) collective-permute-start(f32[3,10,1,128]{3,2,1,0:T(1,128)S(1)} %get-tuple-element.13), channel_id=1, source_target_pairs={{0,1},{1,2},{2,3},{3,0},{4,5},{5,6},{6,7},{7,4},{8,9},{9,10},{10,1... | collective-permute-start | bytes 46088 | tf_op jit(solution)/shard_map/ppermute | solution.py:14
where the time goes:
time: 391 us; the launch traced here: 390 us
  local copies, waits for them, and re-layouts  175 us (45%)
  other arithmetic  159 us (41%)
  blocking collectives  37.7 us (10%)
  starting transfers between devices  13.2 us (3%)
    scatter-add x1, other arithmetic, body(): jnp.zeros((4, total_cells), jnp.float32).at[:, targets]  62.9 us
    sub x2, other arithmetic, body(): corrected = (1.0 - totals[3]) * flat_vel - totals[:3]  54.5 us
    slice x1, local copies, waits for them, and re-layouts, body(): center[0:1] * (east_side - west_side) * 0.5  52.5 us
    gather x2, local copies, waits for them, and re-layouts, body(): jnp.take(flat_vel, src_cell[0, 0].reshape(-1), axis=1)  44.6 us
    psum x1, blocking collectives, body(): points_x = lax.psum(sampled[0], ('gx', 'gy'))  37.7 us
    scatter-add x1, other arithmetic, body(): forcing = jnp.zeros((components, total_cells), jnp.float32).at[:, blade_c...  37.5 us
    reshape x1, local copies, waits for them, and re-layouts, body(): field_now = corrected.reshape(components, cells_x, cells_y, levels)  19.5 us
    reshape x1, local copies, waits for them, and re-layouts, body(): forcing_field = forcing.reshape(components, cells_x, cells_y, levels)  19.5 us
  transfers between devices with their start and end apart: 8, of which 2 were waited for; matrix products, arithmetic and copies ran while one was open for 33% of the time, Pallas kernels for 0%

commit v1 on v0

--- a/solution.py
+++ b/solution.py
@@ -2,6 +2,10 @@
 import jax.numpy as jnp
 from jax import lax
 from jax.sharding import PartitionSpec as P
+
+
+def direct_the_lane(message):
+    return lax.all_gather(message, axis_name=("gx", "gy")).sum(axis=0)
 
 
 def padded_2(cells, sides, width):
@@ -35,7 +39,7 @@
     owned = (blade_tile == my_tile)[None]
     sampled = jnp.where(owned, sampled, jnp.zeros_like(sampled))
     points = blade_cell.shape[1]
-    points_x = lax.psum(sampled[0], ("gx", "gy"))
+    points_x = direct_the_lane(sampled[0])
     rotor_mean = jnp.sum(points_x, axis=1) / points
     forces = -blade_coef[None] * rotor_mean[None, :, None] * sampled
     forcing = (

time: 391 us -> 391 us (level)
  blocking collectives: 37.7 us -> 42.1 us
  starting transfers between devices: 13.2 us -> 9.06 us
    all_gather x0 -> x1, blocking collectives: none -> 42.1 us  [direct_the_lane(): return lax.all_gather(message, axis_name=('gx', 'gy')).sum(axis=0)]
    psum x1 -> x0, blocking collectives: 37.7 us -> none  [body(): points_x = lax.psum(sampled[0], ('gx', 'gy'))]
where the time goes in v1:
time: 391 us; the launch traced here: 390 us
  local copies, waits for them, and re-layouts  175 us (45%)
  other arithmetic  159 us (41%)
  blocking collectives  42.1 us (11%)
  starting transfers between devices  9.06 us (2%)
    scatter-add x1, other arithmetic, body(): jnp.zeros((4, total_cells), jnp.float32).at[:, targets]  62.9 us
    sub x2, other arithmetic, body(): corrected = (1.0 - totals[3]) * flat_vel - totals[:3]  54.5 us
    slice x1, local copies, waits for them, and re-layouts, body(): center[0:1] * (east_side - west_side) * 0.5  52.5 us
    gather x2, local copies, waits for them, and re-layouts, body(): jnp.take(flat_vel, src_cell[0, 0].reshape(-1), axis=1)  44.6 us
    all_gather x1, blocking collectives, direct_the_lane(): return lax.all_gather(message, axis_name=('gx', 'gy')).sum(axis=0)  42.1 us
    scatter-add x1, other arithmetic, body(): forcing = jnp.zeros((components, total_cells), jnp.float32).at[:, blade_c...  37.5 us
    reshape x1, local copies, waits for them, and re-layouts, body(): field_now = corrected.reshape(components, cells_x, cells_y, levels)  19.5 us
    reshape x1, local copies, waits for them, and re-layouts, body(): forcing_field = forcing.reshape(components, cells_x, cells_y, levels)  19.5 us
  transfers between devices with their start and end apart: 8, of which 2 were waited for; matrix products, arithmetic and copies ran while one was open for 33% of the time, Pallas kernels for 0%

profile of v1, /device:TPU:1, one launch (start us, length us, event | category | flops | bytes accessed | tf_op | source)
XLA Modules:
  0.0 390.1 jit_solution(1563077099298250468)
XLA Ops:
  0.6 17.6 %copy.45 = f32[3,8,64,128]{0,3,2,1:T(8,128)} copy(f32[3,8,64,128]{3,2,1,0:T(8,128)} %param.8) | data formatting | bytes 1572864 | tf_op args[0]
  18.3 41.5 %gather_fusion = f32[9216,3]{1,0:T(8,128)} fusion(f32[3,65536]{0,1:T(8,128)} %bitcast.36, s32[9216]{0:T(1024)S(1)} %broadcast_clamp_fusion), kind=kCustom, calls=%fused_computation | custom fusion | bytes 258048 | tf_op jit(solution)/shard_map/jit(_take)/gather | solution.py:53
  59.8 3.1 copy.46
  63.5 0.7 reduce.16
  64.7 2.1 collective-permute-start
  66.8 3.1 collective-permute-start.1
  70.1 16.8 %gather_fusion.1 = f32[3840,3]{1,0:T(8,128)S(1)} fusion(f32[3,65536]{0,1:T(8,128)} %bitcast.37, s32[4096]{0:T(1024)S(1)} %pad_clamp_fusion), kind=kCustom, calls=%fused_computation.1 | custom fusion | bytes 107520 | tf_op jit(solution)/shard_map/jit(_take)/gather | solution.py:38
  86.9 0.9 copy.54
  87.8 42.1 %all_gather.3 = f32[32,20,192]{2,1,0:T(8,128)S(1)} all-gather(f32[1,20,192]{2,1,0:T(8,128)S(1)} %fusion.16), channel_id=1, replica_groups=mesh['gx'=8,'gy'=4] {'gx','gy'}, dimensions={0}, use_global_device_ids=true | all-gather | bytes 506880 | tf_op jit(solution)/shard_map/all_gather | solution.py:8
  131.3 0.6 collective-permute-done.2
  131.8 2.7 collective-permute-done.3
  134.7 3.0 copy.47
  137.7 62.9 %scatter_custom_fusion = f32[4,65536]{0,1:T(8,128)} fusion(s32[9216]{0:T(1024)S(1)} %bitcast.50, f32[9216,4]{1,0:T(8,128)} %copy.47, f32[]{:T(128)} %constant.18.clone.1), kind=kCustom, calls=%fused_computation.12 | custom fusion | flops 36864 | bytes 1049088 | tf_op jit(solution)/shard_map/scatter-add | solution.py:59
  200.6 20.3 %fusion = f32[65536]{0:T(1024)S(1)} fusion(f32[4,65536]{0,1:T(8,128)} %scatter_custom_fusion), kind=kLoop, calls=%fused_computation.9 | loop fusion | flops 65536 | bytes 524288 | tf_op jit(solution)/shard_map/sub | solution.py:60
  220.9 34.2 %slice_subtract_fusion = f32[3,65536]{0,1:T(8,128)} fusion(f32[4,65536]{0,1:T(8,128)} %scatter_custom_fusion, f32[65536]{0:T(1024)S(1)} %fusion, f32[3,8,64,128]{0,3,2,1:T(8,128)} %copy.45), kind=kLoop, calls=%fused_computation.7 | loop fusion | flops 393216 | bytes 2621440 | tf_op jit(solution)/shard_map/sub | solution.py:60
  255.1 19.5 %copy.57 = f32[3,8,64,128]{3,2,1,0:T(8,128)S(1)} copy(f32[3,8,64,128]{0,3,2,1:T(8,128)} %bitcast.35) | data formatting | bytes 1572864 | tf_op jit(solution)/shard_map/reshape | solution.py:61
  274.7 1.5 collective-permute-start.5
  276.2 37.5 %scatter_custom_fusion.1 = f32[3,65536]{0,1:T(8,128)} fusion(s32[3840]{0:T(1024)S(1)} %fusion.17, f32[]{:T(128)} %constant.18.clone.1, f32[3840,3]{1,0:T(8,128)S(1)} %gather_fusion.1, f32[]{:T(128)} %constant.22.clone.1, f32[3840]{0:T(1024)S(1)} %mul.117, pred[3840]{0:T(1024)(128)(4,1)S(1)} %broadcast_in_dim.77, pred[3840]{0:T(1024)(128)(4,1)S(1)} %broadcast_in_dim.75), kind=kCustom, calls=%fused_computation.10 | custom fusion | flops 46080 | bytes 2778624 | tf_op jit(solution)/shard_map/scatter-add | solution.py:48
  313.7 19.5 %copy.56 = f32[3,8,64,128]{3,2,1,0:T(8,128)S(1)} copy(f32[3,8,64,128]{0,3,2,1:T(8,128)} %bitcast.38) | data formatting | bytes 1572864 | tf_op jit(solution)/shard_map/reshape | solution.py:79
  333.2 0.8 collective-permute-start.6
  334.0 1.0 collective-permute-start.7
  335.0 52.5 %slice_reduce_fusion.2 = (f32[65536]{0:T(1024)S(1)}, f32[65536]{0:T(1024)S(1)}, f32[65536]{0:T(1024)S(1)}) fusion(f32[3,65536]{0,1:T(8,128)} %slice_subtract_fusion), kind=kLoop, calls=%fused_computation.6 | loop fusion | bytes 1572864 | tf_op jit(solution)/shard_map/slice | solution.py:75
  387.5 0.8 select_maximum_fusion
  388.3 1.8 multiply_add_fusion
  (58 shorter events, 2.9 us)
Async XLA Ops:
  0.6 17.6 %copy-start.2 = (s32[1,1,9,1024]{3,1,2,0:T(1,128)S(1)}, s32[1,1,9,1024]{3,1,2,0:T(1,128)}, u32[]{:S(2)}) copy-start(s32[1,1,9,1024]{3,1,2,0:T(1,128)} %param.10) | copy-start | bytes 110596
  18.2 45.3 %copy-start.7 = (s32[1,1,9]{2,1,0:T(1,128)S(1)}, s32[1,1,9]{2,1,0:T(1,128)}, u32[]{:S(2)}) copy-start(s32[1,1,9]{2,1,0:T(1,128)} %param.9) | copy-start | bytes 112
  18.2 46.0 %copy-start.3 = (f32[1,1,9,1024]{3,1,2,0:T(1,128)S(1)}, f32[1,1,9,1024]{3,1,2,0:T(1,128)}, u32[]{:S(2)}) copy-start(f32[1,1,9,1024]{3,1,2,0:T(1,128)} %param.11) | copy-start | bytes 110596
  18.2 51.7 %copy-start.4 = (s32[1,1,9,1024]{3,1,2,0:T(1,128)S(1)}, s32[1,1,9,1024]{3,1,2,0:T(1,128)}, u32[]{:S(2)}) copy-start(s32[1,1,9,1024]{3,1,2,0:T(1,128)} %param.12) | copy-start | bytes 110596
  18.2 51.8 %copy-start.1 = (s32[20,192]{1,0:T(8,128)S(1)}, s32[20,192]{1,0:T(8,128)}, u32[]{:S(2)}) copy-start(s32[20,192]{1,0:T(8,128)} %param.14) | copy-start | bytes 46084
  59.8 28.0 %copy-start.6 = (s32[20,192]{1,0:T(8,128)S(1)}, s32[20,192]{1,0:T(8,128)}, u32[]{:S(2)}) copy-start(s32[20,192]{1,0:T(8,128)} %param.13) | copy-start | bytes 46084
  59.8 71.0 %copy-start.5 = (f32[20,192]{1,0:T(8,128)S(1)}, f32[20,192]{1,0:T(8,128)}, u32[]{:S(2)}) copy-start(f32[20,192]{1,0:T(8,128)} %param.15) | copy-start | bytes 46084
  64.7 65.4 %collective-permute-start = (f32[4,1,3,1024]{3,0,2,1:T(4,128)S(1)}, f32[4,1,3,1024]{3,0,2,1:T(4,128)S(1)}, u32[]{:S(2)}, u32[]{:S(2)}) collective-permute-start(f32[4,1,3,1024]{3,0,2,1:T(4,128)S(1)} %get-tuple-element.19), channel_id=1, source_target_pairs={{0,4},{4,8},{8,12},{12,16},{16,20},{20,24},{24,28},{28,0},{1,5},{5... | collective-permute-start | bytes 147464 | tf_op jit(solution)/shard_map/ppermute | solution.py:18
  66.8 63.4 %collective-permute-start.1 = (f32[4,1,3,1024]{3,0,2,1:T(4,128)S(1)}, f32[4,1,3,1024]{3,0,2,1:T(4,128)S(1)}, u32[]{:S(2)}, u32[]{:S(2)}) collective-permute-start(f32[4,1,3,1024]{3,0,2,1:T(4,128)S(1)} %get-tuple-element.20), channel_id=1, source_target_pairs={{4,0},{8,4},{12,8},{16,12},{20,16},{24,20},{28,24},{0,28},{5,1},{9... | collective-permute-start | bytes 147464 | tf_op jit(solution)/shard_map/ppermute | solution.py:20
  130.3 1.5 collective-permute-start.2
  130.3 4.2 %collective-permute-start.3 = (f32[4,5,1,1024]{3,0,2,1:T(4,128)S(1)}, f32[4,5,1,1024]{3,0,2,1:T(4,128)S(1)}, u32[]{:S(2)}, u32[]{:S(2)}) collective-permute-start(f32[4,5,1,1024]{3,0,2,1:T(4,128)S(1)} %get-tuple-element.18), channel_id=1, source_target_pairs={{1,0},{2,1},{3,2},{0,3},{5,4},{6,5},{7,6},{4,7},{9,8},{10,9},{11,1... | collective-permute-start | bytes 245768 | tf_op jit(solution)/shard_map/ppermute | solution.py:20
  274.6 58.5 %collective-permute-start.4 = (f32[3,1,64,128]{3,2,1,0:T(8,128)S(1)}, f32[3,1,64,128]{3,2,1,0:T(8,128)S(1)}, u32[]{:S(2)}, u32[]{:S(2)}) collective-permute-start(f32[3,1,64,128]{3,2,1,0:T(8,128)S(1)} %get-tuple-element.16), channel_id=1, source_target_pairs={{4,0},{8,4},{12,8},{16,12},{20,16},{24,20},{28,24},{0,28},{5,1},{9... | collective-permute-start | bytes 294920 | tf_op jit(solution)/shard_map/ppermute | solution.py:20
  274.7 58.5 %collective-permute-start.5 = (f32[3,1,64,128]{3,2,1,0:T(8,128)S(1)}, f32[3,1,64,128]{3,2,1,0:T(8,128)S(1)}, u32[]{:S(2)}, u32[]{:S(2)}) collective-permute-start(f32[3,1,64,128]{3,2,1,0:T(8,128)S(1)} %get-tuple-element.15), channel_id=1, source_target_pairs={{0,4},{4,8},{8,12},{12,16},{16,20},{20,24},{24,28},{28,0},{1,5},{5... | collective-permute-start | bytes 294920 | tf_op jit(solution)/shard_map/ppermute | solution.py:18
  333.1 55.2 %copy-start = (f32[3,8,64,128]{3,2,1,0:T(8,128)}, f32[3,8,64,128]{3,2,1,0:T(8,128)S(1)}, u32[]{:S(2)}) copy-start(f32[3,8,64,128]{3,2,1,0:T(8,128)S(1)} %copy.56) | copy-start | bytes 2359300
  333.2 54.3 %collective-permute-start.6 = (f32[3,10,1,128]{3,2,1,0:T(1,128)S(1)}, f32[3,10,1,128]{3,2,1,0:T(1,128)S(1)}, u32[]{:S(2)}, u32[]{:S(2)}) collective-permute-start(f32[3,10,1,128]{3,2,1,0:T(1,128)S(1)} %get-tuple-element.14), channel_id=1, source_target_pairs={{1,0},{2,1},{3,2},{0,3},{5,4},{6,5},{7,6},{4,7},{9,8},{10,9},{11,1... | collective-permute-start | bytes 46088 | tf_op jit(solution)/shard_map/ppermute | solution.py:20
  334.0 53.5 %collective-permute-start.7 = (f32[3,10,1,128]{3,2,1,0:T(1,128)S(1)}, f32[3,10,1,128]{3,2,1,0:T(1,128)S(1)}, u32[]{:S(2)}, u32[]{:S(2)}) collective-permute-start(f32[3,10,1,128]{3,2,1,0:T(1,128)S(1)} %get-tuple-element.13), channel_id=1, source_target_pairs={{0,1},{1,2},{2,3},{3,0},{4,5},{5,6},{6,7},{7,4},{8,9},{9,10},{10,1... | collective-permute-start | bytes 46088 | tf_op jit(solution)/shard_map/ppermute | solution.py:18
